TPU v7x, 256 devices: a whole 4x4x8 slice. The times are simulated.
256 devices in a mesh: row: 16 (over z_lo, x, core), col: 16 (over z_hi, y).
Axes of the slice: x: 4, y: 4, z: 8 (z_hi: 4, z_lo: 2; z = z_hi * 2 + z_lo), core: 2. Of those that a mesh axis runs over, the one named last changes fastest.
Arguments:
- embeddings: bfloat16 [32768, 768], P(('row', 'col')), may hold values from -400 to 400
- tile_list: int32 [16, 16, 32, 2], P('row', 'col'), may hold values from -1 to 15, as said below
- seeds: int32 [32768], P(('row', 'col')), may hold values from 0 to 127
Outputs:
- scores: float32 [32768, 64], P(('row', 'col'))
Inputs may be any that keep to these rules, and one draw needn't show every extreme that they name: tile_list[r, c] lists the tiles of the device at row index r and column index c: a live slot (a, b) stands for the tile of document block r * 16 + a against block b * 16 + c, with a < 16, b < 16 and r * 16 + a <= b * 16 + c. Live slots come first and are distinct, empty slots hold -1 in both entries, the tile (c, r) of a block against itself is always listed, and some device fills all 32 slots. `seeds`: values of 64 or more mark a document without a seed label.
All inputs are finite; a program needn't handle non-finite values.
Results may differ from a plain program's by a relative error of at most 0.00056.
Values may be sent and summed in bfloat16 or wider, within the bound.
No kernel may reach another device: no remote copies, remote signals or barrier semaphores. Data moves between devices by JAX's collectives and lax.ppermute only.
A program may use at most 64 MiB of HBM per device.

v0:
```python
import jax
import jax.numpy as jnp
from jax import lax
from jax.sharding import PartitionSpec as P

CLASSES = 64
ITERS = 3
BLEND = 0.8
EPSILON = 1e-06


def slot_table(picks, slot_alive, extent):
    hits = picks[None, :] == jnp.arange(extent, dtype=jnp.int32)[:, None]
    return (hits & slot_alive[None, :]).astype(jnp.float32)


def settle(to_rows, to_cols, col_index):
    col_share = lax.psum_scatter(to_cols, "row", scatter_dimension=0, tiled=True)
    own_block = lax.dynamic_slice_in_dim(to_rows, col_index, 1, 0) + col_share
    placed = lax.dynamic_update_slice_in_dim(to_rows, own_block, col_index, 0)
    return lax.psum(placed, "col")


def local(embeddings, tile_list, seeds):
    row_index = lax.axis_index("row")
    col_index = lax.axis_index("col")
    row_devices = lax.axis_size("row")
    col_devices = lax.axis_size("col")
    row_count, feat_width = embeddings.shape
    sharpness = feat_width**0.5
    highest = lax.Precision.HIGHEST
    features = embeddings.astype(jnp.float32)
    normed = (
        features * lax.rsqrt(jnp.sum(features * features, axis=1, keepdims=True) + EPSILON)
    ).astype(jnp.bfloat16)
    normed_rows = lax.all_gather(normed, "col", axis=0, tiled=True).reshape(
        col_devices, row_count, feat_width
    )
    normed_cols = lax.all_gather(normed, "row", axis=0, tiled=True).reshape(
        row_devices, row_count, feat_width
    )
    slot_pairs = tile_list.reshape(-1, 2)
    slot_total = slot_pairs.shape[0]
    slot_alive = slot_pairs[:, 0] >= 0
    row_pick = jnp.maximum(slot_pairs[:, 0], 0)
    col_pick = jnp.maximum(slot_pairs[:, 1], 0)
    slot_count = jnp.sum(slot_alive.astype(jnp.int32))
    diagonal = jnp.eye(row_count, dtype=bool)

    def build_group(group_index, kernels):
        offset = group_index * 8
        rows_now = lax.dynamic_slice_in_dim(row_pick, offset, 8)
        cols_now = lax.dynamic_slice_in_dim(col_pick, offset, 8)
        alive_now = lax.dynamic_slice_in_dim(slot_alive, offset, 8)
        scores = jnp.einsum(
            "sie,sje->sij",
            normed_rows[rows_now],
            normed_cols[cols_now],
            preferred_element_type=jnp.float32,
        )
        kernel = jnp.exp(sharpness * (scores - 1.0))
        self_pair = (rows_now == col_index) & (cols_now == row_index)
        masked = self_pair[:, None, None] & diagonal[None] | ~alive_now[:, None, None]
        kernel = jnp.where(masked, 0.0, kernel)
        return lax.dynamic_update_slice_in_dim(kernels, kernel, offset, 0)

    kernels = lax.fori_loop(
        0,
        (slot_count + 7) // 8,
        build_group,
        jnp.zeros((slot_total, row_count, row_count), jnp.float32),
    )
    row_table = slot_table(row_pick, slot_alive, col_devices)
    col_table = slot_table(col_pick, slot_alive, row_devices)
    degree = settle(
        jnp.dot(row_table, jnp.sum(kernels, axis=2), precision=highest),
        jnp.dot(col_table, jnp.sum(kernels, axis=1), precision=highest),
        col_index,
    )
    weight = lax.rsqrt(degree)[:, :, None]
    seeded = (seeds[:, None] == jnp.arange(CLASSES, dtype=jnp.int32)[None, :]).astype(jnp.float32)
    seeded = lax.all_gather(seeded, "col", axis=0, tiled=True).reshape(
        col_devices, row_count, CLASSES
    )
    labels = seeded
    for sweep in range(ITERS):
        spread = weight * labels
        own_spread = lax.dynamic_index_in_dim(spread, col_index, 0, keepdims=False)
        col_labels = lax.all_gather(own_spread, "row", axis=0, tiled=True).reshape(
            row_devices, row_count, CLASSES
        )
        to_rows = jnp.einsum("sij,sjc->sic", kernels, col_labels[col_pick], precision=highest)
        to_cols = jnp.einsum("sij,sic->sjc", kernels, spread[row_pick], precision=highest)
        summed = settle(
            jnp.einsum("as,sic->aic", row_table, to_rows, precision=highest),
            jnp.einsum("bs,sjc->bjc", col_table, to_cols, precision=highest),
            col_index,
        )
        labels = BLEND * weight * summed + (1.0 - BLEND) * seeded
    labels = lax.dynamic_index_in_dim(labels, col_index, 0, keepdims=False)
    return CLASSES * labels


def solution(mesh):
    return jax.shard_map(
        local,
        mesh=mesh,
        in_specs=(P(("row", "col"), None), P("row", "col", None, None), P(("row", "col"))),
        out_specs=P(("row", "col"), None),
        check_vma=False,
    )
```

profile of v0, /device:TPU:2, one launch (start us, length us, event | category | flops | bytes accessed | tf_op | source)
XLA Modules:
  0.0 957.5 jit_solution(11870929973664269903)
XLA Ops:
  6.5 1.1 fusion.18
  7.6 1.7 fusion.19
  10.2 1.3 convert_reduce_fusion
  12.8 58.1 %all_gather.20 = f32[2048,64]{0,1:T(8,128)S(1)} all-gather(f32[128,64]{0,1:T(8,128)S(1)} %fusion.21), channel_id=1, replica_groups=mesh['row'=16,'col'=16] {'col'}, dimensions={0}, use_global_device_ids=true | all-gather | bytes 557056 | tf_op jit(solution)/shard_map/all_gather | solution.py:82
  71.7 10.6 %all-gather.6.cloned.1.call-done = bf16[2048,768]{1,0:T(8,128)(2,1)} async-done(((bf16[128,768]{1,0:T(8,128)(2,1)}), bf16[2048,768]{1,0:T(8,128)(2,1)}) %all-gather.6.cloned.1.call-update) | async-done | bytes 3145744 | tf_op jit(solution)/shard_map/all_gather | solution.py:36
  82.3 37.9 %all-gather.8.cloned.1.call-done = bf16[2048,768]{1,0:T(8,128)(2,1)} async-done(((bf16[128,768]{1,0:T(8,128)(2,1)}), bf16[2048,768]{1,0:T(8,128)(2,1)}) %all-gather.8.cloned.1.call-update) | async-done | bytes 3145744 | tf_op jit(solution)/shard_map/all_gather | solution.py:39
  120.4 40.6 %while.13 = (s32[]{:T(128)}, f32[32,128,128]{2,1,0:T(8,128)S(1)}, s32[]{:T(128)}, s32[32]{0:T(128)S(1)}, s32[]{:T(128)}, /*index=5*/s32[32]{0:T(128)S(1)}, s32[]...) while((s32[]{:T(128)}, f32[32,128,128]{2,1,0:T(8,128)S(1)}, ...), condition=%wide.region_3.4_spmd.clone, body=%wide.region_2.3_spmd.clone.sunk | while | flops 202000464 | bytes 10003999 | solution.py:67
  120.6 3.7 gather_fusion
  124.3 3.8 gather_fusion.1
  128.1 2.5 fusion.81
  130.8 3.7 gather_fusion
  134.5 3.8 gather_fusion.1
  138.2 2.5 fusion.81
  140.9 3.7 gather_fusion
  144.6 3.8 gather_fusion.1
  148.4 2.5 fusion.81
  151.1 3.7 gather_fusion
  154.7 3.8 gather_fusion.1
  158.5 2.5 fusion.81
  161.8 24.1 %all-reduce = f32[16,128]{1,0:T(8,128)S(1)} all-reduce(f32[16,128]{1,0:T(8,128)S(1)} %fusion.28), channel_id=5, replica_groups=mesh['row'=16,'col'=16] {'row'}, use_global_device_ids=true, to_apply=%region_6.7.clone | all-reduce | flops 2048 | bytes 16384
  186.7 45.6 %psum.28 = f32[16,128]{1,0:T(8,128)S(1)} all-reduce(f32[16,128]{1,0:T(8,128)S(1)} %dynamic_update_slice.18), channel_id=1, replica_groups=mesh['row'=16,'col'=16] {'col'}, use_global_device_ids=true, to_apply=%region_7.8 | all-reduce | flops 2048 | bytes 16384 | tf_op jit(solution)/shard_map/psum | solution.py:21
  232.4 0.8 copy-done.1
  233.4 1.6 gather_fusion.3
  235.0 3.2 fusion.55
  238.2 1.1 fusion.14
  239.3 0.9 copy.14
  240.3 1.0 constant_dynamic-slice_fusion.3
  241.3 21.8 %all-gather = f32[1,2048,64]{1,0,2:T(1,128)S(1)} all-gather(f32[1,128,64]{1,0,2:T(1,128)S(1)} %constant_dynamic-slice_fusion.3), channel_id=2, replica_groups=mesh['row'=16,'col'=16] {'row'}, dimensions={1}, use_global_device_ids=true | all-gather | bytes 557056 | tf_op jit(solution)/shard_map/all_gather | solution.py:89
  263.2 1.6 gather_fusion.2
  264.8 5.4 fusion.54
  270.2 1.1 fusion.16
  271.3 28.0 %reduce-scatter.4.cloned.1.call-done = f32[1,128,64]{1,2,0:T(8,128)} async-done(((f32[16,128,64]{1,2,0:T(8,128)}), f32[1,128,64]{1,2,0:T(8,128)}) %reduce-scatter.4.cloned.1.call-update) | async-done | bytes 32784 | tf_op jit(solution)/shard_map/reduce_scatter | solution.py:18
  299.2 0.8 dynamic-slice_add_fusion.3
  301.2 168.8 %all-reduce.5.cloned.1.call-done = f32[16,128,64]{1,0,2:T(8,128)} async-done(((f32[16,128,64]{1,0,2:T(8,128)}), f32[16,128,64]{1,0,2:T(8,128)}) %all-reduce.5.cloned.1.call-update) | async-done | bytes 524304 | tf_op jit(solution)/shard_map/psum | solution.py:21
  470.0 1.1 add_multiply_fusion.1
  471.2 0.8 copy-done
  472.1 1.6 gather_fusion.5
  473.7 3.2 fusion.57
  476.9 1.1 fusion.10
  478.0 0.9 copy.20
  479.0 1.0 constant_dynamic-slice_fusion.2
  480.0 17.9 %all-gather.1 = f32[1,2048,64]{1,0,2:T(1,128)S(1)} all-gather(f32[1,128,64]{1,0,2:T(1,128)S(1)} %constant_dynamic-slice_fusion.2), channel_id=3, replica_groups=mesh['row'=16,'col'=16] {'row'}, dimensions={1}, use_global_device_ids=true | all-gather | bytes 557056 | tf_op jit(solution)/shard_map/all_gather | solution.py:89
  498.1 1.6 gather_fusion.4
  499.6 5.4 fusion.56
  505.0 1.1 fusion.12
  506.1 31.8 %reduce-scatter.6.cloned.1.call-done = f32[1,128,64]{1,2,0:T(8,128)} async-done(((f32[16,128,64]{1,2,0:T(8,128)}), f32[1,128,64]{1,2,0:T(8,128)}) %reduce-scatter.6.cloned.1.call-update) | async-done | bytes 32784 | tf_op jit(solution)/shard_map/reduce_scatter | solution.py:18
  537.9 0.8 dynamic-slice_add_fusion.2
  538.8 0.8 copy-done.5
  539.7 169.3 %all-reduce.7.cloned.1.call-done = f32[16,128,64]{1,0,2:T(8,128)} async-done(((f32[16,128,64]{1,0,2:T(8,128)}), f32[16,128,64]{1,0,2:T(8,128)}) %all-reduce.7.cloned.1.call-update) | async-done | bytes 524304 | tf_op jit(solution)/shard_map/psum | solution.py:21
  709.0 1.9 add_multiply_fusion
  711.0 0.8 copy-done.2
  711.9 1.6 gather_fusion.7
  713.5 3.2 fusion.59
  716.7 1.1 fusion.6
  717.8 1.0 copy.26
  718.8 1.0 constant_dynamic-slice_fusion.1
  719.8 18.1 %all-gather.2 = f32[1,2048,64]{1,0,2:T(1,128)S(1)} all-gather(f32[1,128,64]{1,0,2:T(1,128)S(1)} %constant_dynamic-slice_fusion.1), channel_id=4, replica_groups=mesh['row'=16,'col'=16] {'row'}, dimensions={1}, use_global_device_ids=true | all-gather | bytes 557056 | tf_op jit(solution)/shard_map/all_gather | solution.py:89
  738.1 1.6 gather_fusion.6
  739.7 5.4 fusion.58
  745.0 1.1 fusion.8
  746.1 31.6 %reduce-scatter.8.cloned.1.call-done = f32[1,128,64]{1,2,0:T(8,128)} async-done(((f32[16,128,64]{1,2,0:T(8,128)}), f32[1,128,64]{1,2,0:T(8,128)}) %reduce-scatter.8.cloned.1.call-update) | async-done | bytes 32784 | tf_op jit(solution)/shard_map/reduce_scatter | solution.py:18
  777.7 0.8 dynamic-slice_add_fusion.1
  779.5 169.5 %all-reduce.9.cloned.1.call-done = f32[16,128,64]{1,0,2:T(8,128)} async-done(((f32[16,128,64]{1,0,2:T(8,128)}), f32[16,128,64]{1,0,2:T(8,128)}) %all-reduce.9.cloned.1.call-update) | async-done | bytes 524304 | tf_op jit(solution)/shard_map/psum | solution.py:21
  948.9 1.7 fusion.20
  (74 shorter events, 8.4 us)
Async XLA Ops:
  6.5 64.5 %copy-start.7 = (u32[256]{0:T(256)S(1)}, u32[256]{0:T(256)}, u32[]{:S(2)}) copy-start(u32[256]{0:T(256)} %constant.99) | copy-start | bytes 3076
  6.5 65.2 %copy-start.6 = (s32[1,1,32,2]{2,3,1,0:T(2,128)S(1)}, s32[1,1,32,2]{2,3,1,0:T(2,128)}, u32[]{:S(2)}) copy-start(s32[1,1,32,2]{2,3,1,0:T(2,128)} %param.6) | copy-start | bytes 772
  6.5 75.7 %all-gather.6.cloned.1.call-start = ((), (), s32[]{:S(2)}) async-start(), calls=%async_computation.3 | async-start | bytes 3342336 | tf_op jit(solution)/shard_map/all_gather | solution.py:36
  9.4 110.8 %all-gather.8.cloned.1.call-start = ((), (), s32[]{:S(2)}) async-start(), calls=%async_computation.4 | async-start | bytes 3342336 | tf_op jit(solution)/shard_map/all_gather | solution.py:39
  10.1 289.1 %reduce-scatter.4.cloned.1.call-start = ((), (), s32[]{:S(2)}) async-start(), calls=%async_computation.5 | async-start | bytes 557056 | tf_op jit(solution)/shard_map/reduce_scatter | solution.py:18
  232.4 0.8 copy-start.1
  240.2 229.8 %all-reduce.5.cloned.1.call-start = ((), (), s32[]{:S(2)}) async-start(), calls=%async_computation.6 | async-start | bytes 1048576 | tf_op jit(solution)/shard_map/psum | solution.py:21
  300.2 0.8 copy-start.4
  301.0 236.9 %reduce-scatter.6.cloned.1.call-start = ((), (), s32[]{:S(2)}) async-start(), calls=%async_computation.7 | async-start | bytes 557056 | tf_op jit(solution)/shard_map/reduce_scatter | solution.py:18
  471.2 0.8 copy-start
  478.9 230.1 %all-reduce.7.cloned.1.call-start = ((), (), s32[]{:S(2)}) async-start(), calls=%async_computation.8 | async-start | bytes 1048576 | tf_op jit(solution)/shard_map/psum | solution.py:21
  538.8 0.8 copy-start.5
  539.6 238.1 %reduce-scatter.8.cloned.1.call-start = ((), (), s32[]{:S(2)}) async-start(), calls=%async_computation.9 | async-start | bytes 557056 | tf_op jit(solution)/shard_map/reduce_scatter | solution.py:18
  711.0 0.8 copy-start.2
  718.7 230.2 %all-reduce.9.cloned.1.call-start = ((), (), s32[]{:S(2)}) async-start(), calls=%async_computation.10 | async-start | bytes 1048576 | tf_op jit(solution)/shard_map/psum | solution.py:21
  778.7 0.8 copy-start.3
Sparse Core Ops, SparseCore 0:
  9.8 72.4 all-gather.5
  84.1 36.0 all-gather.7
  240.3 58.8 reduce-scatter.3
  301.7 168.3 all-reduce.4
  479.1 58.7 reduce-scatter.5
  540.4 168.6 all-reduce.6
  718.9 58.7 reduce-scatter.7
  780.3 168.5 all-reduce.8
where the time goes:
time: 959 us; the launch traced here: 957 us
  waiting for transfers between devices  648 us (68%)
  blocking collectives  186 us (19%)
  local copies, waits for them, and re-layouts  52.3 us (5%)
  matrix products  42.2 us (4%)
  between operations  14.5 us (2%)
  other arithmetic  14.1 us (1%)
    psum x3, waiting for transfers between devices, settle(): return lax.psum(placed, 'col')  508 us
    reduce_scatter x3, waiting for transfers between devices, settle(): lax.psum_scatter(to_cols, 'row', scatter_dimension=0, tiled=True)  91.3 us
    all_gather x1, blocking collectives, local(): lax.all_gather(seeded, 'col', axis=0, tiled=True)  58.1 us
    all_gather x3, blocking collectives, local(): lax.all_gather(own_spread, 'row', axis=0, tiled=True)  57.8 us
    psum x1, blocking collectives, settle(): return lax.psum(placed, 'col')  45.6 us
    all_gather x1, waiting for transfers between devices, local(): lax.all_gather(normed, 'row', axis=0, tiled=True)  37.9 us
    unnamed x1, blocking collectives  24.1 us
  transfers between devices with their start and end apart: 8, of which 8 were waited for; matrix products, arithmetic and copies ran while one was open for 3% of the time, Pallas kernels for 0%

commit v1 on v0

--- a/solution.py
+++ b/solution.py
@@ -18,7 +18,7 @@
     col_share = lax.psum_scatter(to_cols, "row", scatter_dimension=0, tiled=True)
     own_block = lax.dynamic_slice_in_dim(to_rows, col_index, 1, 0) + col_share
     placed = lax.dynamic_update_slice_in_dim(to_rows, own_block, col_index, 0)
-    return lax.psum(placed, "col")
+    return jnp.sum(lax.all_gather(placed, "col"), axis=0)
 
 
 def local(embeddings, tile_list, seeds):

time: 959 us -> 821 us (0.86); the launches traced: 957 us -> 805 us
  waiting for transfers between devices: 648 us -> 457 us
  blocking collectives: 186 us -> 214 us
  other arithmetic: 14.1 us -> 29.6 us
    psum x3 -> x0, waiting for transfers between devices: 508 us -> none  [settle(): return lax.psum(placed, 'col')]
    all_gather x0 -> x3, waiting for transfers between devices: none -> 317 us  [settle(): return jnp.sum(lax.all_gather(placed, 'col'), axis=0)]
    psum x1 -> x0, blocking collectives: 45.6 us -> none  [settle(): return lax.psum(placed, 'col')]
    all_gather x0 -> x1, blocking collectives: none -> 44.7 us  [settle(): return jnp.sum(lax.all_gather(placed, 'col'), axis=0)]
    all_gather x3, blocking collectives: 57.8 us -> 86.3 us  [local(): lax.all_gather(own_spread, 'row', axis=0, tiled=True)]
    reduce_sum x0 -> x4, other arithmetic: none -> 14.4 us  [settle(): return jnp.sum(lax.all_gather(placed, 'col'), axis=0)]
  transfers between devices with their start and end apart: 8 -> 8, of which waited for: 8 -> 8; matrix products, arithmetic and copies ran while one was open for 3% -> 4% of each run, Pallas kernels for 0% -> 0%
where the time goes in v1:
time: 821 us; the launch traced here: 805 us
  waiting for transfers between devices  457 us (56%)
  blocking collectives  214 us (26%)
  local copies, waits for them, and re-layouts  48.3 us (6%)
  matrix products  42.2 us (5%)
  other arithmetic  29.6 us (4%)
  between operations  14.4 us (2%)
    all_gather x3, waiting for transfers between devices, settle(): return jnp.sum(lax.all_gather(placed, 'col'), axis=0)  317 us
    reduce_scatter x3, waiting for transfers between devices, settle(): lax.psum_scatter(to_cols, 'row', scatter_dimension=0, tiled=True)  92 us
    all_gather x3, blocking collectives, local(): lax.all_gather(own_spread, 'row', axis=0, tiled=True)  86.3 us
    all_gather x1, blocking collectives, local(): lax.all_gather(seeded, 'col', axis=0, tiled=True)  58.5 us
    all_gather x1, blocking collectives, settle(): return jnp.sum(lax.all_gather(placed, 'col'), axis=0)  44.7 us
    all_gather x1, waiting for transfers between devices, local(): lax.all_gather(normed, 'row', axis=0, tiled=True)  38.8 us
    unnamed x1, blocking collectives  24.1 us
  transfers between devices with their start and end apart: 8, of which 8 were waited for; matrix products, arithmetic and copies ran while one was open for 4% of the time, Pallas kernels for 0%

profile of v1, /device:TPU:2, one launch (start us, length us, event | category | flops | bytes accessed | tf_op | source)
XLA Modules:
  0.0 805.5 jit_solution(1998639542384619762)
XLA Ops:
  6.5 1.0 fusion.18
  7.6 1.7 fusion.19
  10.1 1.3 convert_reduce_fusion
  12.1 1.3 dynamic-slice
  15.6 58.5 %all_gather.55 = f32[2048,64]{0,1:T(8,128)S(1)} all-gather(f32[128,64]{0,1:T(8,128)S(1)} %fusion.22), channel_id=1, replica_groups=mesh['row'=16,'col'=16] {'col'}, dimensions={0}, use_global_device_ids=true | all-gather | bytes 557056 | tf_op jit(solution)/shard_map/all_gather | solution.py:82
  74.1 7.9 all-gather.9.cloned.1.call-done
  82.0 38.8 %all-gather.11.cloned.1.call-done = bf16[2048,768]{1,0:T(8,128)(2,1)} async-done(((bf16[128,768]{1,0:T(8,128)(2,1)}), bf16[2048,768]{1,0:T(8,128)(2,1)}) %all-gather.11.cloned.1.call-update) | async-done | bytes 3145744 | tf_op jit(solution)/shard_map/all_gather | solution.py:39
  121.0 40.6 %while.13 = (s32[]{:T(128)}, f32[32,128,128]{2,1,0:T(8,128)S(1)}, s32[]{:T(128)}, s32[32]{0:T(128)S(1)}, s32[]{:T(128)}, /*index=5*/s32[32]{0:T(128)S(1)}, s32[]...) while((s32[]{:T(128)}, f32[32,128,128]{2,1,0:T(8,128)S(1)}, ...), condition=%wide.region_3.4_spmd.clone, body=%wide.region_2.3_spmd.clone.sunk | while | flops 202000464 | bytes 10003999 | solution.py:67
  121.2 3.7 gather_fusion
  124.9 3.8 gather_fusion.1
  128.7 2.5 fusion.86
  131.4 3.7 gather_fusion
  135.1 3.8 gather_fusion.1
  138.8 2.5 fusion.86
  141.5 3.7 gather_fusion
  145.2 3.8 gather_fusion.1
  149.0 2.5 fusion.86
  151.7 3.7 gather_fusion
  155.4 3.8 gather_fusion.1
  159.1 2.5 fusion.86
  162.4 24.1 %all-reduce = f32[16,128]{1,0:T(8,128)S(1)} all-reduce(f32[16,128]{1,0:T(8,128)S(1)} %fusion.29), channel_id=5, replica_groups=mesh['row'=16,'col'=16] {'row'}, use_global_device_ids=true, to_apply=%region_6.7.clone | all-reduce | flops 2048 | bytes 16384
  187.3 44.7 %all_gather.54 = f32[16,16,128]{2,1,0:T(8,128)S(1)} all-gather(f32[1,16,128]{2,1,0:T(8,128)S(1)} %dynamic_update_slice.22), channel_id=1, replica_groups=mesh['row'=16,'col'=16] {'col'}, dimensions={0}, use_global_device_ids=true | all-gather | bytes 139264 | tf_op jit(solution)/shard_map/all_gather | solution.py:21
  232.1 1.6 gather_fusion.3
  233.7 3.2 fusion.57
  236.9 1.1 fusion.14
  238.0 1.0 copy.28
  239.1 21.8 %all-gather = f32[1,2048,64]{1,2,0:T(8,128)S(1)} all-gather(f32[1,128,64]{1,2,0:T(8,128)S(1)} %constant_dynamic-slice_fusion.3), channel_id=2, replica_groups=mesh['row'=16,'col'=16] {'row'}, dimensions={1}, use_global_device_ids=true | all-gather | bytes 557056 | tf_op jit(solution)/shard_map/all_gather | solution.py:89
  261.1 1.6 gather_fusion.2
  262.7 5.4 fusion.56
  268.1 1.1 fusion.16
  269.2 28.6 %reduce-scatter.4.cloned.1.call-done = f32[1,128,64]{1,2,0:T(8,128)} async-done(((f32[16,128,64]{1,2,0:T(8,128)}), f32[1,128,64]{1,2,0:T(8,128)}) %reduce-scatter.4.cloned.1.call-update) | async-done | bytes 32784 | tf_op jit(solution)/shard_map/reduce_scatter | solution.py:18
  297.7 0.8 add_bitcast_fusion.2
  298.7 1.0 copy.31
  299.9 105.5 %all-gather.13.cloned.1.call-done = f32[16,16,128,64]{2,3,1,0:T(8,128)} async-done(((f32[1,16,128,64]{2,3,1,0:T(8,128)}), f32[16,16,128,64]{2,3,1,0:T(8,128)}) %all-gather.13.cloned.1.call-update) | async-done | bytes 8388624 | tf_op jit(solution)/shard_map/all_gather | solution.py:21
  405.4 5.1 reduce_sum.77
  410.5 1.1 add_multiply_fusion.1
  411.6 1.6 gather_fusion.5
  413.2 3.2 fusion.59
  416.4 1.1 fusion.10
  417.5 1.0 copy.38
  418.6 32.3 %all-gather.1 = f32[1,2048,64]{1,2,0:T(8,128)S(1)} all-gather(f32[1,128,64]{1,2,0:T(8,128)S(1)} %constant_dynamic-slice_fusion.2), channel_id=3, replica_groups=mesh['row'=16,'col'=16] {'row'}, dimensions={1}, use_global_device_ids=true | all-gather | bytes 557056 | tf_op jit(solution)/shard_map/all_gather | solution.py:89
  451.1 1.6 gather_fusion.4
  452.7 5.4 fusion.58
  458.1 1.1 fusion.12
  459.2 31.7 %reduce-scatter.6.cloned.1.call-done = f32[1,128,64]{1,2,0:T(8,128)} async-done(((f32[16,128,64]{1,2,0:T(8,128)}), f32[1,128,64]{1,2,0:T(8,128)}) %reduce-scatter.6.cloned.1.call-update) | async-done | bytes 32784 | tf_op jit(solution)/shard_map/reduce_scatter | solution.py:18
  490.9 0.8 add_bitcast_fusion.1
  491.8 1.0 copy.41
  493.1 105.6 %all-gather.15.cloned.1.call-done = f32[16,16,128,64]{2,3,1,0:T(8,128)} async-done(((f32[1,16,128,64]{2,3,1,0:T(8,128)}), f32[16,16,128,64]{2,3,1,0:T(8,128)}) %all-gather.15.cloned.1.call-update) | async-done | bytes 8388624 | tf_op jit(solution)/shard_map/all_gather | solution.py:21
  598.7 5.1 reduce_sum.78
  603.8 2.0 add_multiply_fusion
  605.8 1.6 gather_fusion.7
  607.4 3.2 fusion.61
  610.6 1.1 fusion.6
  611.7 1.0 copy.47
  612.7 32.3 %all-gather.2 = f32[1,2048,64]{1,2,0:T(8,128)S(1)} all-gather(f32[1,128,64]{1,2,0:T(8,128)S(1)} %constant_dynamic-slice_fusion.1), channel_id=4, replica_groups=mesh['row'=16,'col'=16] {'row'}, dimensions={1}, use_global_device_ids=true | all-gather | bytes 557056 | tf_op jit(solution)/shard_map/all_gather | solution.py:89
  645.3 1.6 gather_fusion.6
  646.9 5.4 fusion.60
  652.3 1.1 fusion.8
  653.3 31.7 %reduce-scatter.8.cloned.1.call-done = f32[1,128,64]{1,2,0:T(8,128)} async-done(((f32[16,128,64]{1,2,0:T(8,128)}), f32[1,128,64]{1,2,0:T(8,128)}) %reduce-scatter.8.cloned.1.call-update) | async-done | bytes 32784 | tf_op jit(solution)/shard_map/reduce_scatter | solution.py:18
  685.0 0.8 add_bitcast_fusion
  686.0 1.0 copy.50
  687.1 106.0 %all-gather.17.cloned.1.call-done = f32[16,16,128,64]{2,3,1,0:T(8,128)} async-done(((f32[1,16,128,64]{2,3,1,0:T(8,128)}), f32[16,16,128,64]{2,3,1,0:T(8,128)}) %all-gather.17.cloned.1.call-update) | async-done | bytes 8388624 | tf_op jit(solution)/shard_map/all_gather | solution.py:21
  793.0 4.2 reduce_sum.79
  797.3 1.4 fusion.21
  (64 shorter events, 7.6 us)
Async XLA Ops:
  6.5 75.5 %all-gather.9.cloned.1.call-start = ((), (), s32[]{:S(2)}) async-start(), calls=%async_computation.3 | async-start | bytes 3342336 | tf_op jit(solution)/shard_map/all_gather | solution.py:36
  9.3 111.5 %all-gather.11.cloned.1.call-start = ((), (), s32[]{:S(2)}) async-start(), calls=%async_computation.4 | async-start | bytes 3342336 | tf_op jit(solution)/shard_map/all_gather | solution.py:39
  10.1 287.7 %reduce-scatter.4.cloned.1.call-start = ((), (), s32[]{:S(2)}) async-start(), calls=%async_computation.5 | async-start | bytes 557056 | tf_op jit(solution)/shard_map/reduce_scatter | solution.py:18
  239.0 166.5 %all-gather.13.cloned.1.call-start = ((), (), s32[]{:S(2)}) async-start(), calls=%async_computation.6 | async-start | bytes 8912896 | tf_op jit(solution)/shard_map/all_gather | solution.py:21
  299.7 191.2 %reduce-scatter.6.cloned.1.call-start = ((), (), s32[]{:S(2)}) async-start(), calls=%async_computation.7 | async-start | bytes 557056 | tf_op jit(solution)/shard_map/reduce_scatter | solution.py:18
  418.5 180.2 %all-gather.15.cloned.1.call-start = ((), (), s32[]{:S(2)}) async-start(), calls=%async_computation.8 | async-start | bytes 8912896 | tf_op jit(solution)/shard_map/all_gather | solution.py:21
  492.9 192.2 %reduce-scatter.8.cloned.1.call-start = ((), (), s32[]{:S(2)}) async-start(), calls=%async_computation.9 | async-start | bytes 557056 | tf_op jit(solution)/shard_map/reduce_scatter | solution.py:18
  612.7 180.4 %all-gather.17.cloned.1.call-start = ((), (), s32[]{:S(2)}) async-start(), calls=%async_computation.10 | async-start | bytes 8912896 | tf_op jit(solution)/shard_map/all_gather | solution.py:21
Sparse Core Ops, SparseCore 0:
  9.8 72.1 all-gather.8
  83.8 36.9 all-gather.10
  239.1 58.5 reduce-scatter.3
  300.0 105.3 all-gather.12
  418.6 72.2 reduce-scatter.5
  493.2 105.5 all-gather.14
  612.8 72.2 reduce-scatter.7
  687.5 105.5 all-gather.16
